TPU v7x, 512 devices: a whole 4x4x16 slice. The times are simulated.
512 devices in a mesh: ctx: 64 (over x, z), ch: 8 (over y, core).
Axes of the slice: x: 4, y: 4, z: 16, core: 2. Of those that a mesh axis runs over, the one named last changes fastest.
Arguments:
- q_proj: bfloat16 [16384, 4096], P('ctx', 'ch'), may hold values from -6 to 6
- k_proj: bfloat16 [16384, 4096], P('ctx', 'ch'), may hold values from -6 to 6
- v_proj: bfloat16 [16384, 4096], P('ctx', 'ch'), may hold values from -6 to 6
- residue: float32 [16, 4096], P(None, 'ch'), may hold values from -4 to 4
- rate: float32 [16, 4096], P(None, 'ch'), may hold values from 1.2207031e-05 to 0.1
- skip: float32 [4096], P('ch'), may hold values from -4 to 4
- w_out: bfloat16 [4096, 6144], P('ctx', 'ch'), may hold values from -0.09375 to 0.09375
Outputs:
- mixed: bfloat16 [16384, 6144], P('ctx', 'ch')
All inputs are finite; a program needn't handle non-finite values.
Results may differ from a plain program's by a relative error of at most 0.0049.
Values may be sent and summed in bfloat16 or wider, within the bound.
A program may use at most 128 MiB of HBM per device.

v0:
```python
import jax
import jax.numpy as jnp
from jax import lax
from jax.sharding import PartitionSpec as P


def carried_in(part, axis, combine, identity):
    place = lax.axis_index(axis)
    gathered = jax.tree.map(lambda a: lax.all_gather(a, axis), part)
    state = jax.tree.map(lambda a, e: jnp.zeros_like(a) + jnp.asarray(e, a.dtype), part, identity)

    def one(turn, state):
        return combine(
            state, jax.tree.map(lambda a: lax.dynamic_index_in_dim(a, turn, 0, False), gathered)
        )

    return lax.fori_loop(0, place, one, state)


def compose(earlier, later):
    return (earlier[0] * later[0], later[0] * earlier[1] + later[1])


def body(q_proj, k_proj, v_proj, residue, rate, skip, w_out):
    highest = lax.Precision.HIGHEST
    tok_rows, chan_count = q_proj.shape
    signal = k_proj.astype(jnp.float32) * v_proj.astype(jnp.float32)
    sub_len = min(64, tok_rows // 4)
    sub_count = tok_rows // sub_len
    pieces = signal.reshape(sub_count, sub_len, chan_count)
    lag_steps = jnp.arange(sub_len).astype(jnp.float32)
    powers = jnp.exp(-rate[:, None, :] * lag_steps[None, :, None])
    coefficient = residue * jnp.sqrt(2.0 * rate)
    filter_taps = jnp.einsum("mc,mkc->kc", coefficient, powers, precision=highest)
    offsets = jnp.arange(sub_len)[:, None] - jnp.arange(sub_len)[None, :]
    toeplitz = jnp.where(
        (offsets >= 0)[:, :, None], filter_taps[jnp.clip(offsets, 0, sub_len - 1)], 0.0
    )
    local_part = jnp.einsum("tsc,bsc->btc", toeplitz, pieces, precision=highest)
    ends = jnp.einsum("msc,bsc->bmc", powers[:, ::-1, :], pieces, precision=highest)
    sub_index = jnp.arange(sub_count)
    sub_gap = sub_index[:, None] - 1 - sub_index[None, :]
    gap_float = jnp.maximum(sub_gap, 0).astype(jnp.float32)
    within = jnp.where(
        (sub_gap >= 0)[:, :, None, None],
        jnp.exp(-(rate * sub_len)[None, None] * gap_float[:, :, None, None]),
        0.0,
    )
    inner = jnp.einsum("bamc,amc->bmc", within, ends, precision=highest)
    sub_decay = jnp.exp(-rate * sub_len)
    total_end = sub_decay * inner[-1] + ends[-1]
    dev_decay = jnp.exp(-rate * tok_rows)
    prefix = carried_in(
        (dev_decay, total_end),
        "ctx",
        compose,
        (jnp.ones_like(dev_decay), jnp.zeros_like(total_end)),
    )
    entering = prefix[1]
    start_powers = jnp.exp(-(rate * sub_len)[None] * sub_index.astype(jnp.float32)[:, None, None])
    arriving = inner + start_powers * entering[None]
    reach = coefficient[:, None, :] * powers * jnp.exp(-rate)[:, None, :]
    carried = jnp.einsum("mtc,bmc->btc", reach, arriving, precision=highest)
    conv = (local_part + carried).reshape(tok_rows, chan_count) + skip[None, :] * signal
    gated = (q_proj.astype(jnp.float32) * conv).astype(jnp.bfloat16)
    full_gated = lax.all_gather(gated, "ch", axis=1, tiled=True)
    mixed = jnp.dot(
        full_gated,
        lax.all_gather(w_out, "ctx", axis=0, tiled=True),
        preferred_element_type=jnp.float32,
    )
    return mixed.astype(jnp.bfloat16)


def solution(mesh):
    placed = (
        P("ctx", "ch"),
        P("ctx", "ch"),
        P("ctx", "ch"),
        P(None, "ch"),
        P(None, "ch"),
        P("ch"),
        P("ctx", "ch"),
    )
    return jax.shard_map(
        body, mesh=mesh, in_specs=placed, out_specs=P("ctx", "ch"), check_vma=False
    )
```

profile of v0, /device:TPU:32, one launch (start us, length us, event | category | flops | bytes accessed | tf_op | source)
XLA Modules:
  0.0 568.6 jit_solution(16598735904272384695)
XLA Ops:
  6.5 0.0 all-gather.11.cloned.1.call-start
  6.5 0.1 maximum_convert_fusion
  6.6 0.1 fusion.21
  6.7 1.1 convert_multiply_fusion
  7.8 0.4 copy.49
  8.2 0.8 multiply_negate_fusion
  9.0 0.1 copy.47
  9.1 3.6 multiply_exponential_fusion
  12.7 7.3 %rev.3 = f32[16,64,512]{1,0,2:T(8,128)} reverse(f32[16,64,512]{1,0,2:T(8,128)} %multiply_exponential_fusion), dimensions={1} | reverse | bytes 4194304 | tf_op jit(solution)/shard_map/rev | solution.py:40
  20.0 0.0 copy-start
  20.0 0.0 copy-start.1
  20.0 8.4 %fusion.23 = f32[512,4,16]{2,1,0:T(4,128)S(1)} fusion(f32[4,64,512]{1,0,2:T(4,128)S(1)} %copy.49, f32[16,64,512]{1,0,2:T(8,128)} %rev.3), kind=kOutput, calls=%fused_computation.43 | convolution fusion | flops 25165824 | bytes 2752512 | tf_op jit(solution)/shard_map/msc,bsc->bmc/dot_general | solution.py:40
  28.3 0.3 copy.73
  28.6 0.2 multiply_reduce_fusion.1
  28.8 0.0 copy-done
  28.9 0.0 copy-done.1
  28.9 0.7 negate_exponential_fusion
  29.5 0.0 all-gather.11.cloned.1.call-update
  29.5 0.0 all-gather.13.cloned.1.call-start
  29.6 0.7 all-gather.13.cloned.1.call-update
  30.3 0.2 all-gather.7.cloned.1.call-start
  30.5 0.8 copy.52
  31.4 0.1 copy.71
  31.5 6.0 %multiply_reduce_fusion = f32[512,64]{1,0:T(8,128)S(1)} fusion(f32[512,16]{1,0:T(8,128)S(1)} %copy.71, f32[64]{0:T(128)S(1)} %iota_convert_fusion.1, f32[16,512]{0,1:T(8,128)S(1)} %copy.47), kind=kLoop, calls=%fused_computation.7 | loop fusion | flops 1540096 | bytes 196864
  37.5 0.1 copy.61
  37.6 0.1 reshape.112
  37.7 16.8 %gather_fusion = f32[4096,512]{1,0:T(8,128)} fusion(f32[64,512]{1,0:T(8,128)S(1)} %bitcast.54, s32[4096]{0:T(1024)S(1)} %broadcast_clamp_fusion), kind=kCustom, calls=%fused_computation | custom fusion | bytes 16793600 | tf_op jit(solution)/shard_map/gather | solution.py:37
  54.5 16.3 %copy.48 = f32[64,64,512]{1,0,2:T(8,128)} copy(f32[64,64,512]{2,1,0:T(8,128)} %bitcast.55) | data formatting | bytes 16777216 | tf_op jit(solution)/shard_map/gather | solution.py:37
  70.8 0.8 copy.53
  71.7 29.0 %fusion = f32[512,4,64]{2,1,0:T(4,128)S(1)} fusion(f32[4,64,512]{1,0,2:T(4,128)S(1)} %copy.49, f32[64,64,512]{1,0,2:T(8,128)} %copy.48, pred[64,64]{1,0:T(8,128)(4,1)S(1)} %subtract_compare_fusion), kind=kOutput, calls=%fused_computation.3 | convolution fusion | flops 102760448 | bytes 9441280 | tf_op jit(solution)/shard_map/tsc,bsc->btc/dot_general | solution.py:39
  100.7 74.2 %all-gather.11.cloned.1.call-done = f32[1024,512]{1,0:T(8,128)} async-done(((f32[16,512]{1,0:T(8,128)}), f32[1024,512]{1,0:T(8,128)}) %all-gather.11.cloned.1.call-update) | async-done | bytes 2097168 | tf_op jit(solution)/shard_map/all_gather | solution.py:9
  174.9 139.8 %all-gather.13.cloned.1.call-done = f32[1024,512]{1,0:T(8,128)} async-done(((f32[16,512]{1,0:T(8,128)}), f32[1024,512]{1,0:T(8,128)}) %all-gather.13.cloned.1.call-update) | async-done | bytes 2097168 | tf_op jit(solution)/shard_map/all_gather | solution.py:9
  314.7 0.8 while.12
  314.7 0.8 bitcast_add_fusion.3
  315.5 0.1 multiply_add_fusion
  315.6 0.4 copy.54
  316.0 0.0 copy-start.2
  316.0 8.4 %fusion.14 = f32[4,64,512]{1,0,2:T(4,128)S(1)} fusion(f32[512,4,64]{2,1,0:T(4,128)S(1)} %fusion, f32[4,16,512]{1,0,2:T(4,128)S(1)} %copy.54, f32[16,512]{0,1:T(8,128)} %copy.53, f32[16,512]{0,1:T(8,128)} %copy.52, f32[64]{0:T(128)S(1)} %iota_convert_fusion.1, f32[16,512]{0,1:T(8,128)S(1)} %copy.47), kind=kOutput, calls=%fused_computation.17 | convolution fusion | flops 26869760 | bytes 1278208 | tf_op jit(solution)/shard_map/mtc,bmc->btc/dot_general | solution.py:63
  324.5 0.3 copy.55
  324.8 0.0 copy-done.2
  324.9 2.0 fusion.18
  326.8 0.0 all-gather.7.cloned.1.call-update
  326.8 0.0 all-gather.9.cloned.1.call-start
  326.9 0.5 all-gather.9.cloned.1.call-update
  327.4 74.4 %all-gather.7.cloned.1.call-done = bf16[256,4096]{1,0:T(8,128)(2,1)} async-done(((bf16[256,512]{1,0:T(8,128)(2,1)}), bf16[256,4096]{1,0:T(8,128)(2,1)}) %all-gather.7.cloned.1.call-update) | async-done | bytes 2097168 | tf_op jit(solution)/shard_map/all_gather | solution.py:66
  401.8 154.3 %all-gather.9.cloned.1.call-done = bf16[4096,768]{1,0:T(8,128)(2,1)} async-done(((bf16[64,768]{1,0:T(8,128)(2,1)}), bf16[4096,768]{1,0:T(8,128)(2,1)}) %all-gather.9.cloned.1.call-update) | async-done | bytes 6291472 | tf_op jit(solution)/shard_map/all_gather | solution.py:69
  556.2 6.0 %convolution_convert_fusion = bf16[256,768]{1,0:T(8,128)(2,1)} fusion(bf16[256,4096]{1,0:T(8,128)(2,1)} %all-gather.7.cloned.1.call-done, bf16[4096,768]{1,0:T(8,128)(2,1)} %all-gather.9.cloned.1.call-done), kind=kOutput, calls=%fused_computation.18 | convolution fusion | flops 1610809344 | bytes 8781824 | tf_op jit(solution)/shard_map/dot_general | solution.py:67
  (7 shorter events, 0.0 us)
Async XLA Ops:
  6.5 168.4 %all-gather.11.cloned.1.call-start = ((), (), s32[]{:S(2)}) async-start(), calls=%async_computation.2 | async-start | bytes 2129920 | tf_op jit(solution)/shard_map/all_gather | solution.py:9
  20.0 8.9 %copy-start = (f32[16,512]{1,0:T(8,128)S(1)}, f32[16,512]{1,0:T(8,128)}, u32[]{:S(2)}) copy-start(f32[16,512]{1,0:T(8,128)} %param.13) | copy-start | bytes 98308
  20.0 8.9 %copy-start.1 = (f32[16,512]{1,0:T(8,128)S(1)}, f32[16,512]{1,0:T(8,128)}, u32[]{:S(2)}) copy-start(f32[16,512]{1,0:T(8,128)} %param.12) | copy-start | bytes 98308
  29.5 285.2 %all-gather.13.cloned.1.call-start = ((), (), s32[]{:S(2)}) async-start(), calls=%async_computation.3 | async-start | bytes 2129920 | tf_op jit(solution)/shard_map/all_gather | solution.py:9
  30.3 371.5 %all-gather.7.cloned.1.call-start = ((), (), s32[]{:S(2)}) async-start(), calls=%async_computation | async-start | bytes 2359296 | tf_op jit(solution)/shard_map/all_gather | solution.py:66
  316.0 8.8 %copy-start.2 = (f32[512]{0:T(512)S(1)}, f32[512]{0:T(512)}, u32[]{:S(2)}) copy-start(f32[512]{0:T(512)} %param.14) | copy-start | bytes 6148
  326.8 229.3 %all-gather.9.cloned.1.call-start = ((), (), s32[]{:S(2)}) async-start(), calls=%async_computation.1 | async-start | bytes 6389760 | tf_op jit(solution)/shard_map/all_gather | solution.py:69
Sparse Core Ops, SparseCore 0:
  29.7 145.1 all-gather.10
  177.8 136.8 all-gather.12
  326.9 74.8 all-gather.6
  404.6 151.4 all-gather.8
where the time goes:
time: 574 us; the launch traced here: 569 us
  waiting for transfers between devices  444 us (77%)
  matrix products  51.7 us (9%)
  local copies, waits for them, and re-layouts  44 us (8%)
  other arithmetic  15.3 us (3%)
  between operations  13.3 us (2%)
    all_gather x2, waiting for transfers between devices, carried_in(): gathered = jax.tree.map(lambda a: lax.all_gather(a, axis), part)  214 us
    all_gather x1, waiting for transfers between devices, body(): lax.all_gather(w_out, 'ctx', axis=0, tiled=True)  154 us
    all_gather x1, waiting for transfers between devices, body(): full_gated = lax.all_gather(gated, 'ch', axis=1, tiled=True)  74.4 us
    gather x2, local copies, waits for them, and re-layouts, body(): filter_taps[jnp.clip(offsets, 0, sub_len - 1)]  33.1 us
    dot_general x1, matrix products, body(): local_part = jnp.einsum('tsc,bsc->btc', toeplitz, pieces, precision=highest)  29 us
  transfers between devices with their start and end apart: 4, of which 4 were waited for; matrix products, arithmetic and copies ran while one was open for 12% of the time, Pallas kernels for 0%

commit v1 on v0

v1 whole, which is shorter than its diff:
```python
import jax
import jax.numpy as jnp
from jax import lax
from jax.experimental import pallas as pl
from jax.experimental.pallas import tpu as pltpu
from jax.sharding import PartitionSpec as P

MESH = pl.DeviceIdType.MESH
NX, NZ, NY, NC = 4, 16, 4, 2
ROWS, CH, MODES = 256, 512, 16
WROWS, COLS, PCOLS = 64, 768, 256
GROUPS, CHUNKS, LEN = 4, 8, 32
PR, PL, QR, QL = 8, 7, 7, 8
PS, QS = pl.ds(0, PCOLS), pl.ds(PCOLS, COLS - PCOLS)
F32, BF16 = jnp.float32, jnp.bfloat16


def kernel(
    q_hbm, k_hbm, v_hbm, w_hbm, residue, rate, skip, out,
    q, k, v, w, a, sig, y_buf, carry, acc, decay, coef,
    ends, got_ends, totals, states, got_states, pref,
    load_sem, st_send, st_recv, w_send, w_recv, a_send, a_recv,
):
    ctx, ch = lax.axis_index("ctx"), lax.axis_index("ch")
    x, z = ctx // NZ, ctx % NZ
    y, core = ch // NC, ch % NC
    xp, xm, x2 = (x + 1) % NX, (x + 3) % NX, (x + 2) % NX
    zp, zm = (z + 1) % NZ, (z + NZ - 1) % NZ
    yp, ym, y2 = (y + 1) % NY, (y + 3) % NY, (y + 2) % NY

    def at(x_to=None, z_to=None, ch_to=None):
        x_to = x if x_to is None else x_to
        z_to = z if z_to is None else z_to
        return (x_to * NZ + z_to, ch if ch_to is None else ch_to)

    def remote(src, dst, send, recv, where):
        return pltpu.make_async_remote_copy(
            src_ref=src, dst_ref=dst, send_sem=send, recv_sem=recv,
            device_id=where, device_id_type=MESH,
        )

    loads = [
        pltpu.make_async_copy(k_hbm, k, load_sem.at[0]),
        pltpu.make_async_copy(v_hbm, v, load_sem.at[1]),
        pltpu.make_async_copy(w_hbm, w.at[z, x], load_sem.at[2]),
        pltpu.make_async_copy(q_hbm, q, load_sem.at[3]),
    ]
    for c in loads:
        c.start()

    barrier = pltpu.get_barrier_semaphore()
    greet = [at(z_to=(z + i) % NZ) for i in range(1, NZ)]
    greet += [at(x_to=t) for t in (xp, xm, x2)]
    greet += [at(ch_to=yp * NC + core), at(ch_to=ym * NC + core), at(ch_to=y * NC + 1 - core)]
    for d in greet:
        pl.semaphore_signal(barrier, inc=1, device_id=d, device_id_type=MESH)

    decay[...] = jnp.exp(-rate[...])
    coef[...] = residue[...] * jnp.sqrt(2.0 * rate[...])
    loads[0].wait()
    loads[1].wait()
    chunk = lax.broadcasted_iota(jnp.int32, (CHUNKS, 128), 0)
    chunk_f = chunk.astype(F32)

    def rows_of(ref, m, lanes):
        return jnp.broadcast_to(ref[m : m + 1, lanes], (CHUNKS, 128))

    def shifted(val, n):
        return jnp.where(chunk >= n, pltpu.roll(val, n, 0), 0.0)

    for g in range(GROUPS):
        lanes = slice(g * 128, (g + 1) * 128)
        sig[g] = k[:, lanes].astype(F32) * v[:, lanes].astype(F32)
        ds = [rows_of(decay, m, lanes) for m in range(MODES)]

        def scan1(o, hs, g=g, ds=ds):
            for u in range(4):
                s = sig[g, pl.ds(o * 4 + u, CHUNKS, stride=LEN), :]
                hs = [d * h + s for d, h in zip(ds, hs)]
            return hs

        hs = lax.fori_loop(0, LEN // 4, scan1, [jnp.zeros((CHUNKS, 128), F32)] * MODES)
        for m in range(MODES):
            r = rows_of(rate, m, lanes) * float(LEN)
            end = jnp.sum(hs[m] * jnp.exp(-r * (CHUNKS - 1.0 - chunk_f)), axis=0, keepdims=True)
            ends[m, 0:1, lanes] = end
            c1 = jnp.exp(-r)
            val = shifted(hs[m], 1)
            val = val + c1 * shifted(val, 1)
            c2 = c1 * c1
            val = val + c2 * shifted(val, 2)
            val = val + (c2 * c2) * shifted(val, 4)
            carry[g, m] = val

    got_ends[z] = ends[z]
    loads[2].wait()
    pl.semaphore_wait(barrier, len(greet))

    def all_z(src, dst, n):
        def one(i, _):
            to = (z + i) % NZ
            remote(src.at[to], dst.at[z], st_send.at[n], st_recv.at[n], at(z_to=to)).start()
            return 0

        lax.fori_loop(1, NZ, one, 0)

    def settle(ref, count, sem):
        part = ref.at[pl.ds(0, count)]
        pltpu.make_async_copy(part, part, sem).wait()

    all_z(ends, got_ends, 0)

    keys = {}

    def slot(key):
        return keys.setdefault(key, len(keys))

    pending = []

    def w_copy(key, part, where):
        n = slot(key)
        return remote(part, part, w_send.at[n], w_recv.at[n], where)

    def send(key, part, where):
        c = w_copy(key, part, where)
        c.start()
        pending.append(c)

    def arrived(key, part):
        w_copy(key, part, at(z_to=zp)).wait_recv()

    def q_part(z_at, x_at):
        return w.at[z_at, x_at, :, QS]

    def p_part(z_at):
        return w.at[z_at, :, :, PS]

    def back(s):
        return (z + NZ - s) % NZ

    def ahead(s):
        return (z + s) % NZ

    def across(way, s, z_at):
        part = q_part(z_at, x)
        send(("x+", way, s), part, at(x_to=xp))
        send(("x-", way, s), part, at(x_to=xm))

    def relay(way, s):
        if way == "r":
            z_at = back(s)
            part = q_part(z_at, xm)
            arrived(("x+", way, s), part)
            send(("x2", way, s), part, at(x_to=xp))
        else:
            z_at = ahead(s)
            part = q_part(z_at, xp)
            arrived(("x-", way, s), part)
            send(("x2", way, s), part, at(x_to=xm))

    def q_step(s):
        if s <= QR:
            if s:
                arrived(("qr", s - 1), q_part(back(s), x))
            if s < QR:
                send(("qr", s), q_part(back(s), x), at(z_to=zp))
        if s <= QL:
            if s:
                arrived(("ql", s - 1), q_part(ahead(s), x))
            if s < QL:
                send(("ql", s), q_part(ahead(s), x), at(z_to=zm))
        if s <= QR:
            across("r", s, back(s))
        if 0 < s <= QL:
            across("l", s, ahead(s))

    def p_step(s):
        if s <= PR:
            if s:
                arrived(("pr", s - 1), p_part(back(s)))
            if s < PR:
                send(("pr", s), p_part(back(s)), at(z_to=zp))
        if s <= PL:
            if s:
                arrived(("pl", s - 1), p_part(ahead(s)))
            if s < PL:
                send(("pl", s), p_part(ahead(s)), at(z_to=zm))

    def relay_step(s):
        if s <= QR:
            relay("r", s)
        if 0 < s <= QL:
            relay("l", s)

    def w_step(s):
        q_step(s)
        p_step(s)
        relay_step(s - 1)

    q_step(0)
    for key, x_to in (("p+", xp), ("p-", xm), ("p2", x2)):
        send((key,), w.at[z, x, :, PS], at(x_to=x_to))
    for key, x_from in (("p+", xm), ("p-", xp), ("p2", x2)):
        arrived((key,), w.at[z, x_from, :, PS])
    p_step(0)
    w_step(1)

    settle(got_ends, NZ - 1, st_recv.at[0])
    own_rate = rate[pl.ds(z, 1), :]
    step_decay = jnp.exp(-own_rate * float(ROWS))
    total = jnp.zeros((1, CH), F32)
    for i in range(NZ):
        pref[i] = total
        total = step_decay * total + got_ends[i]
    totals[x] = total
    for t in (xp, xm, x2):
        remote(totals.at[x], totals.at[x], st_send.at[1], st_recv.at[1], at(x_to=t)).start()
    w_step(2)
    settle(totals, NX - 1, st_recv.at[1])
    entering = jnp.zeros((1, CH), F32)
    for i in range(NX):
        gap = jnp.maximum(x - 1 - i, 0).astype(F32)
        used = jnp.where(i < x, 1.0, 0.0)
        entering = entering + used * jnp.exp(-own_rate * (float(ROWS * NZ) * gap)) * totals[i]
    for i in range(NZ):
        states[i] = pref[i] + jnp.exp(-own_rate * float(ROWS * i)) * entering
    got_states[z] = states[z]
    all_z(states, got_states, 2)
    w_step(3)
    w_step(4)
    settle(got_states, NZ - 1, st_recv.at[2])
    loads[3].wait()

    a_pending = []
    partner = at(ch_to=y * NC + 1 - core)

    def a_copy(kind, g, block, where):
        part = a.at[block, g]
        return remote(part, part, a_send.at[kind, g], a_recv.at[kind, g], where)

    def a_go(kind, g, block, where):
        c = a_copy(kind, g, block, where)
        c.start()
        a_pending.append(c)

    up, down, far = at(ch_to=yp * NC + core), at(ch_to=ym * NC + core), y2 * NC + core
    from_up, from_down = yp * NC + core, ym * NC + core

    def a_make(g):
        lanes = slice(g * 128, (g + 1) * 128)
        ds = [rows_of(decay, m, lanes) for m in range(MODES)]
        cs = [rows_of(coef, m, lanes) for m in range(MODES)]
        hs = []
        for m in range(MODES):
            r = rows_of(rate, m, lanes) * float(LEN)
            into = jnp.broadcast_to(got_states[m, 0:1, lanes], (CHUNKS, 128))
            hs.append(carry[g, m] + jnp.exp(-r * chunk_f) * into)

        def scan2(o, hs):
            for u in range(2):
                where = pl.ds(o * 2 + u, CHUNKS, stride=LEN)
                s = sig[g, where, :]
                hs = [d * h + s for d, h in zip(ds, hs)]
                terms = [c * h for c, h in zip(cs, hs)]
                while len(terms) > 1:
                    terms = [p + r for p, r in zip(terms[::2], terms[1::2])]
                y_buf[where, :] = terms[0]
            return hs

        lax.fori_loop(0, LEN // 2, scan2, hs)
        conv = y_buf[...] + skip[0:1, lanes] * sig[g]
        a[ch, g] = (q[:, lanes].astype(F32) * conv).astype(BF16)
        a_go(1, g, ch, up)
        a_go(2, g, ch, down)
        a_go(0, g, ch, partner)

    def a_pass(g):
        a_copy(1, g, from_down, up).wait_recv()
        if g % 2 == 0:
            a_go(3, g, from_down, up)
        a_go(4, g, from_down, partner)
        a_copy(2, g, from_up, up).wait_recv()
        if g % 2 == 1:
            a_go(3, g, from_up, down)
        a_go(5, g, from_up, partner)

    def a_last(g):
        a_copy(3, g, far, up).wait_recv()
        a_go(6, g, far, partner)

    a_make(0)
    a_make(1)
    w_step(5)
    a_make(2)
    a_make(3)
    a_pass(0)
    w_step(6)
    a_pass(1)
    a_pass(2)
    a_last(0)
    w_step(7)
    a_pass(3)
    a_last(1)
    a_last(2)
    w_step(8)
    a_last(3)
    relay_step(8)

    for s in range(QR + 1):
        arrived(("x-", "r", s), q_part(back(s), xp))
        arrived(("x2", "r", s), q_part(back(s), x2))
    for s in range(1, QL + 1):
        arrived(("x+", "l", s), q_part(ahead(s), xm))
        arrived(("x2", "l", s), q_part(ahead(s), x2))
    other = 1 - core
    for kind, block in ((0, y), (4, ym), (5, yp), (6, y2)):
        for g in range(GROUPS):
            a_copy(kind, g, block * NC + other, partner).wait_recv()

    def multiply(j, _):
        left = jnp.concatenate([a[j, g] for g in range(GROUPS)], axis=1)
        first, x_at = (j % 2) * 8, j // 2
        for n in range(COLS // 256):
            cols = slice(n * 256, (n + 1) * 256)
            right = w[pl.ds(first, 8), x_at, :, cols].reshape(8 * WROWS, 256)
            acc[:, cols] += jnp.dot(left, right, preferred_element_type=F32)
        return 0

    acc[...] = jnp.zeros_like(acc)
    lax.fori_loop(0, NY * NC, multiply, 0)
    out[...] = acc[...].astype(BF16)

    settle(got_ends, NZ - 1, st_send.at[0])
    settle(totals, NX - 1, st_send.at[1])
    settle(got_states, NZ - 1, st_send.at[2])
    for c in pending + a_pending:
        c.wait_send()


def body(q_proj, k_proj, v_proj, residue, rate, skip, w_out):
    vmem = pl.BlockSpec(memory_space=pltpu.VMEM)
    hbm = pl.BlockSpec(memory_space=pl.ANY)
    dma = pltpu.SemaphoreType.DMA
    n_w = PR + PL + QR + QL + 3 * NZ + 3
    row = (1, CH)
    return pl.pallas_call(
        kernel,
        out_shape=jax.ShapeDtypeStruct((ROWS, COLS), BF16),
        in_specs=[hbm] * 4 + [vmem] * 3,
        out_specs=vmem,
        scratch_shapes=[
            pltpu.VMEM((ROWS, CH), BF16),
            pltpu.VMEM((ROWS, CH), BF16),
            pltpu.VMEM((ROWS, CH), BF16),
            pltpu.VMEM((NZ, NX, WROWS, COLS), BF16),
            pltpu.VMEM((NY * NC, GROUPS, ROWS, 128), BF16),
            pltpu.VMEM((GROUPS, ROWS, 128), F32),
            pltpu.VMEM((ROWS, 128), F32),
            pltpu.VMEM((GROUPS, MODES, CHUNKS, 128), F32),
            pltpu.VMEM((ROWS, COLS), F32),
            pltpu.VMEM((MODES, CH), F32),
            pltpu.VMEM((MODES, CH), F32),
            pltpu.VMEM((MODES,) + row, F32),
            pltpu.VMEM((NZ,) + row, F32),
            pltpu.VMEM((NX,) + row, F32),
            pltpu.VMEM((NZ,) + row, F32),
            pltpu.VMEM((MODES,) + row, F32),
            pltpu.VMEM((NZ,) + row, F32),
            dma((4,)),
            dma((3,)),
            dma((3,)),
            dma((n_w,)),
            dma((n_w,)),
            dma((7, GROUPS)),
            dma((7, GROUPS)),
        ],
        compiler_params=pltpu.CompilerParams(
            collective_id=0, has_side_effects=True, vmem_limit_bytes=48 * 2**20
        ),
    )(q_proj, k_proj, v_proj, w_out, residue, rate, skip.reshape(1, CH))


def solution(mesh):
    placed = (
        P("ctx", "ch"),
        P("ctx", "ch"),
        P("ctx", "ch"),
        P(None, "ch"),
        P(None, "ch"),
        P("ch"),
        P("ctx", "ch"),
    )
    return jax.shard_map(
        body, mesh=mesh, in_specs=placed, out_specs=P("ctx", "ch"), check_vma=False
    )
```

time: 574 us -> 75.8 us (0.13)
  the two profiles are of different devices: /device:TPU:32 before, /device:TPU:4 now
where the time goes in v1:
time: 75.8 us; the launch traced here: 75.4 us
  Pallas kernels  68.7 us (91%)
  local copies, waits for them, and re-layouts  6.68 us (9%)
    pallas_call x1, Pallas kernels, body(): pl.pallas_call(kernel, out_shape=jax.ShapeDtypeStruct((ROWS, COLS), BF16)...  68.7 us
    unnamed x15, local copies, waits for them, and re-layouts  6.68 us

profile of v1, /device:TPU:4, one launch (start us, length us, event | category | flops | bytes accessed | tf_op | source)
XLA Modules:
  0.0 75.4 jit_solution(9451784610232217110)
XLA Ops:
  0.0 0.0 copy-start
  0.0 0.9 %copy-done = bf16[256,512]{1,0:T(8,128)(2,1)S(1)} copy-done((bf16[256,512]{1,0:T(8,128)(2,1)S(1)}, bf16[256,512]{1,0:T(8,128)(2,1)}, u32[]{:S(2)}) %copy-start) | copy-done | bytes 262168
  1.0 0.0 copy-start.1
  1.0 0.9 %copy-done.1 = bf16[256,512]{1,0:T(8,128)(2,1)S(1)} copy-done((bf16[256,512]{1,0:T(8,128)(2,1)S(1)}, bf16[256,512]{1,0:T(8,128)(2,1)}, u32[]{:S(2)}) %copy-start.1) | copy-done | bytes 262168
  1.9 0.0 copy-start.2
  1.9 0.9 %copy-done.2 = bf16[256,512]{1,0:T(8,128)(2,1)S(1)} copy-done((bf16[256,512]{1,0:T(8,128)(2,1)S(1)}, bf16[256,512]{1,0:T(8,128)(2,1)}, u32[]{:S(2)}) %copy-start.2) | copy-done | bytes 262168
  2.9 0.0 copy-start.3
  2.9 0.9 %copy-done.3 = bf16[64,768]{1,0:T(8,128)(2,1)S(1)} copy-done((bf16[64,768]{1,0:T(8,128)(2,1)S(1)}, bf16[64,768]{1,0:T(8,128)(2,1)}, u32[]{:S(2)}) %copy-start.3) | copy-done | bytes 98328
  3.7 0.0 copy-start.4
  3.7 0.8 %copy-done.4 = f32[16,512]{1,0:T(8,128)S(1)} copy-done((f32[16,512]{1,0:T(8,128)S(1)}, f32[16,512]{1,0:T(8,128)}, u32[]{:S(2)}) %copy-start.4) | copy-done | bytes 32792
  4.5 0.0 copy-start.5
  4.5 0.8 %copy-done.5 = f32[16,512]{1,0:T(8,128)S(1)} copy-done((f32[16,512]{1,0:T(8,128)S(1)}, f32[16,512]{1,0:T(8,128)}, u32[]{:S(2)}) %copy-start.5) | copy-done | bytes 32792
  5.3 0.0 copy-start.6
  5.3 0.7 copy-done.6
  5.9 68.7 %shard_map.73 = bf16[256,768]{1,0:T(8,128)(2,1)S(1)} custom-call(bf16[256,512]{1,0:T(8,128)(2,1)S(1)} %copy-done, bf16[256,512]{1,0:T(8,128)(2,1)S(1)} %copy-done.1, bf16[256,512]{1,0:T(8,128)(2,1)S(1)} %copy-done.2, bf16[64,768]{1,0:T(8,128)(2,1)S(1)} %copy-done.3, f32[16,512]{1,0:T(8,128)S(1)} %copy-done.4, f32[16,512]{1,0:T(8,128)S(1)} %copy-done.5, ...), custom_call_target="tpu_custom_call" | custom-call | tf_op jit(solution)/shard_map/pallas_call | solution.py:346
  74.7 0.7 copy.9
Async XLA Ops:
  0.0 0.9 %copy-start = (bf16[256,512]{1,0:T(8,128)(2,1)S(1)}, bf16[256,512]{1,0:T(8,128)(2,1)}, u32[]{:S(2)}) copy-start(bf16[256,512]{1,0:T(8,128)(2,1)} %q_hbm.1) | copy-start | bytes 786436
  1.0 0.9 %copy-start.1 = (bf16[256,512]{1,0:T(8,128)(2,1)S(1)}, bf16[256,512]{1,0:T(8,128)(2,1)}, u32[]{:S(2)}) copy-start(bf16[256,512]{1,0:T(8,128)(2,1)} %k_hbm.1) | copy-start | bytes 786436
  1.9 0.9 %copy-start.2 = (bf16[256,512]{1,0:T(8,128)(2,1)S(1)}, bf16[256,512]{1,0:T(8,128)(2,1)}, u32[]{:S(2)}) copy-start(bf16[256,512]{1,0:T(8,128)(2,1)} %v_hbm.1) | copy-start | bytes 786436
  2.9 0.9 %copy-start.3 = (bf16[64,768]{1,0:T(8,128)(2,1)S(1)}, bf16[64,768]{1,0:T(8,128)(2,1)}, u32[]{:S(2)}) copy-start(bf16[64,768]{1,0:T(8,128)(2,1)} %w_hbm.1) | copy-start | bytes 294916
  3.7 0.8 %copy-start.4 = (f32[16,512]{1,0:T(8,128)S(1)}, f32[16,512]{1,0:T(8,128)}, u32[]{:S(2)}) copy-start(f32[16,512]{1,0:T(8,128)} %residue.1) | copy-start | bytes 98308
  4.5 0.8 %copy-start.5 = (f32[16,512]{1,0:T(8,128)S(1)}, f32[16,512]{1,0:T(8,128)}, u32[]{:S(2)}) copy-start(f32[16,512]{1,0:T(8,128)} %rate.1) | copy-start | bytes 98308
  5.3 0.7 copy-start.6

commit v2 on v1

--- a/solution.py
+++ b/solution.py
@@ -16,8 +16,8 @@
 
 
 def kernel(
-    q_hbm, k_hbm, v_hbm, w_hbm, residue, rate, skip, out,
-    q, k, v, w, a, sig, y_buf, carry, acc, decay, coef,
+    q_hbm, k_hbm, v_hbm, w_hbm, residue_hbm, rate_hbm, skip_hbm, out,
+    q, k, v, residue, rate, skip, w, a, sig, y_buf, carry, acc, decay, coef,
     ends, got_ends, totals, states, got_states, pref,
     load_sem, st_send, st_recv, w_send, w_recv, a_send, a_recv,
 ):
@@ -44,6 +44,9 @@
         pltpu.make_async_copy(v_hbm, v, load_sem.at[1]),
         pltpu.make_async_copy(w_hbm, w.at[z, x], load_sem.at[2]),
         pltpu.make_async_copy(q_hbm, q, load_sem.at[3]),
+        pltpu.make_async_copy(rate_hbm, rate, load_sem.at[4]),
+        pltpu.make_async_copy(residue_hbm, residue, load_sem.at[5]),
+        pltpu.make_async_copy(skip_hbm, skip, load_sem.at[6]),
     ]
     for c in loads:
         c.start()
@@ -55,8 +58,8 @@
     for d in greet:
         pl.semaphore_signal(barrier, inc=1, device_id=d, device_id_type=MESH)
 
+    loads[4].wait()
     decay[...] = jnp.exp(-rate[...])
-    coef[...] = residue[...] * jnp.sqrt(2.0 * rate[...])
     loads[0].wait()
     loads[1].wait()
     chunk = lax.broadcasted_iota(jnp.int32, (CHUNKS, 128), 0)
@@ -230,6 +233,9 @@
     w_step(4)
     settle(got_states, NZ - 1, st_recv.at[2])
     loads[3].wait()
+    loads[5].wait()
+    loads[6].wait()
+    coef[...] = residue[...] * jnp.sqrt(2.0 * rate[...])
 
     a_pending = []
     partner = at(ch_to=y * NC + 1 - core)
@@ -346,12 +352,15 @@
     return pl.pallas_call(
         kernel,
         out_shape=jax.ShapeDtypeStruct((ROWS, COLS), BF16),
-        in_specs=[hbm] * 4 + [vmem] * 3,
+        in_specs=[hbm] * 7,
         out_specs=vmem,
         scratch_shapes=[
             pltpu.VMEM((ROWS, CH), BF16),
             pltpu.VMEM((ROWS, CH), BF16),
             pltpu.VMEM((ROWS, CH), BF16),
+            pltpu.VMEM((MODES, CH), F32),
+            pltpu.VMEM((MODES, CH), F32),
+            pltpu.VMEM(row, F32),
             pltpu.VMEM((NZ, NX, WROWS, COLS), BF16),
             pltpu.VMEM((NY * NC, GROUPS, ROWS, 128), BF16),
             pltpu.VMEM((GROUPS, ROWS, 128), F32),
@@ -366,7 +375,7 @@
             pltpu.VMEM((NZ,) + row, F32),
             pltpu.VMEM((MODES,) + row, F32),
             pltpu.VMEM((NZ,) + row, F32),
-            dma((4,)),
+            dma((7,)),
             dma((3,)),
             dma((3,)),
             dma((n_w,)),
@@ -375,7 +384,7 @@
             dma((7, GROUPS)),
         ],
         compiler_params=pltpu.CompilerParams(
-            collective_id=0, has_side_effects=True, vmem_limit_bytes=48 * 2**20
+            collective_id=0, has_side_effects=True
         ),
     )(q_proj, k_proj, v_proj, w_out, residue, rate, skip.reshape(1, CH))
 

time: 75.8 us -> 71.4 us (0.942)
  local copies, waits for them, and re-layouts: 6.68 us -> 1.77 us
    unnamed x15 -> x1, local copies, waits for them, and re-layouts: 6.68 us -> 1.77 us
where the time goes in v2:
time: 71.4 us; the launch traced here: 71.2 us
  Pallas kernels  69.4 us (97%)
  local copies, waits for them, and re-layouts  1.77 us (2%)
    pallas_call x1, Pallas kernels, body(): pl.pallas_call(kernel, out_shape=jax.ShapeDtypeStruct((ROWS, COLS), BF16)...  69.4 us
    unnamed x1, local copies, waits for them, and re-layouts  1.77 us

profile of v2, /device:TPU:4, one launch (start us, length us, event | category | flops | bytes accessed | tf_op | source)
XLA Modules:
  0.0 71.2 jit_solution(417838549891426297)
XLA Ops:
  0.0 69.4 %shard_map.73 = bf16[256,768]{1,0:T(8,128)(2,1)} custom-call(bf16[256,512]{1,0:T(8,128)(2,1)} %q_hbm.1, bf16[256,512]{1,0:T(8,128)(2,1)} %k_hbm.1, bf16[256,512]{1,0:T(8,128)(2,1)} %v_hbm.1, bf16[64,768]{1,0:T(8,128)(2,1)} %w_hbm.1, f32[16,512]{1,0:T(8,128)} %residue_hbm.1, f32[16,512]{1,0:T(8,128)} %rate_hbm.1, f32[1,512]{1,0:T(1,128)} %bitcast.1), custom_call_target="tpu_custom_call" | custom-call | tf_op jit(solution)/shard_map/pallas_call | solution.py:352
  69.4 1.8 %copy.9 = bf16[256,768]{1,0:T(8,128)(2,1)} copy(bf16[256,768]{1,0:T(8,128)(2,1)} %shard_map.73) | data formatting | bytes 786432

commit v3 on v2

--- a/solution.py
+++ b/solution.py
@@ -11,15 +11,32 @@
 WROWS, COLS, PCOLS = 64, 768, 256
 GROUPS, CHUNKS, LEN = 4, 8, 32
 PR, PL, QR, QL = 8, 7, 7, 8
-PS, QS = pl.ds(0, PCOLS), pl.ds(PCOLS, COLS - PCOLS)
+QCOLS = COLS - PCOLS
 F32, BF16 = jnp.float32, jnp.bfloat16
+EARLY = "".split()
+PLAN = " ".join(
+    (
+        "I0 p0 q1 r0",
+        "p1 E0 q2 r1",
+        "p2 T0 q3 r2",
+        "p3 q4 r3 H0",
+        "m0 p4 m1 q5",
+        "r4 m2 p5 m3",
+        "b0 q6 r5 b1",
+        "p6 b2 l0 q7",
+        "r6 b3 l1 p7",
+        "l2 q8 r7 l3",
+        "p8 r8",
+    )
+).split()
+NEAR = (1, 3, 4, NZ - 4, NZ - 3, NZ - 1)
 
 
 def kernel(
     q_hbm, k_hbm, v_hbm, w_hbm, residue_hbm, rate_hbm, skip_hbm, out,
-    q, k, v, residue, rate, skip, w, a, sig, y_buf, carry, acc, decay, coef,
+    q, k, v, residue, rate, skip, w_p, w_q, a, sig, y_buf, carry, acc, decay, coef,
     ends, got_ends, totals, states, got_states, pref,
-    load_sem, st_send, st_recv, w_send, w_recv, a_send, a_recv,
+    load_sem, known, st_send, st_recv, w_send, w_recv, a_send, a_recv,
 ):
     ctx, ch = lax.axis_index("ctx"), lax.axis_index("ch")
     x, z = ctx // NZ, ctx % NZ
@@ -42,7 +59,8 @@
     loads = [
         pltpu.make_async_copy(k_hbm, k, load_sem.at[0]),
         pltpu.make_async_copy(v_hbm, v, load_sem.at[1]),
-        pltpu.make_async_copy(w_hbm, w.at[z, x], load_sem.at[2]),
+        pltpu.make_async_copy(w_hbm.at[:, pl.ds(0, PCOLS)], w_p.at[z, x], load_sem.at[2]),
+        pltpu.make_async_copy(w_hbm.at[:, pl.ds(PCOLS, QCOLS)], w_q.at[z, x], load_sem.at[7]),
         pltpu.make_async_copy(q_hbm, q, load_sem.at[3]),
         pltpu.make_async_copy(rate_hbm, rate, load_sem.at[4]),
         pltpu.make_async_copy(residue_hbm, residue, load_sem.at[5]),
@@ -52,16 +70,12 @@
         c.start()
 
     barrier = pltpu.get_barrier_semaphore()
-    greet = [at(z_to=(z + i) % NZ) for i in range(1, NZ)]
+    greet = [at(z_to=(z + i) % NZ) for i in NEAR]
     greet += [at(x_to=t) for t in (xp, xm, x2)]
     greet += [at(ch_to=yp * NC + core), at(ch_to=ym * NC + core), at(ch_to=y * NC + 1 - core)]
     for d in greet:
         pl.semaphore_signal(barrier, inc=1, device_id=d, device_id_type=MESH)
 
-    loads[4].wait()
-    decay[...] = jnp.exp(-rate[...])
-    loads[0].wait()
-    loads[1].wait()
     chunk = lax.broadcasted_iota(jnp.int32, (CHUNKS, 128), 0)
     chunk_f = chunk.astype(F32)
 
@@ -71,7 +85,7 @@
     def shifted(val, n):
         return jnp.where(chunk >= n, pltpu.roll(val, n, 0), 0.0)
 
-    for g in range(GROUPS):
+    def first_pass(g):
         lanes = slice(g * 128, (g + 1) * 128)
         sig[g] = k[:, lanes].astype(F32) * v[:, lanes].astype(F32)
         ds = [rows_of(decay, m, lanes) for m in range(MODES)]
@@ -95,9 +109,6 @@
             val = val + (c2 * c2) * shifted(val, 4)
             carry[g, m] = val
 
-    got_ends[z] = ends[z]
-    loads[2].wait()
-    pl.semaphore_wait(barrier, len(greet))
 
     def all_z(src, dst, n):
         def one(i, _):
@@ -111,8 +122,6 @@
         part = ref.at[pl.ds(0, count)]
         pltpu.make_async_copy(part, part, sem).wait()
 
-    all_z(ends, got_ends, 0)
-
     keys = {}
 
     def slot(key):
@@ -133,10 +142,10 @@
         w_copy(key, part, at(z_to=zp)).wait_recv()
 
     def q_part(z_at, x_at):
-        return w.at[z_at, x_at, :, QS]
-
-    def p_part(z_at):
-        return w.at[z_at, :, :, PS]
+        return w_q.at[z_at, x_at]
+
+    def p_part(z_at, half):
+        return w_p.at[z_at, pl.ds(2 * half, 2)]
 
     def back(s):
         return (z + NZ - s) % NZ
@@ -178,16 +187,17 @@
             across("l", s, ahead(s))
 
     def p_step(s):
-        if s <= PR:
-            if s:
-                arrived(("pr", s - 1), p_part(back(s)))
-            if s < PR:
-                send(("pr", s), p_part(back(s)), at(z_to=zp))
-        if s <= PL:
-            if s:
-                arrived(("pl", s - 1), p_part(ahead(s)))
-            if s < PL:
-                send(("pl", s), p_part(ahead(s)), at(z_to=zm))
+        for half in range(2):
+            if s <= PR:
+                if s:
+                    arrived(("pr", s - 1, half), p_part(back(s), half))
+                if s < PR:
+                    send(("pr", s, half), p_part(back(s), half), at(z_to=zp))
+            if s <= PL:
+                if s:
+                    arrived(("pl", s - 1, half), p_part(ahead(s), half))
+                if s < PL:
+                    send(("pl", s, half), p_part(ahead(s), half), at(z_to=zm))
 
     def relay_step(s):
         if s <= QR:
@@ -195,47 +205,41 @@
         if 0 < s <= QL:
             relay("l", s)
 
-    def w_step(s):
-        q_step(s)
-        p_step(s)
-        relay_step(s - 1)
-
-    q_step(0)
-    for key, x_to in (("p+", xp), ("p-", xm), ("p2", x2)):
-        send((key,), w.at[z, x, :, PS], at(x_to=x_to))
-    for key, x_from in (("p+", xm), ("p-", xp), ("p2", x2)):
-        arrived((key,), w.at[z, x_from, :, PS])
-    p_step(0)
-    w_step(1)
-
-    settle(got_ends, NZ - 1, st_recv.at[0])
-    own_rate = rate[pl.ds(z, 1), :]
-    step_decay = jnp.exp(-own_rate * float(ROWS))
-    total = jnp.zeros((1, CH), F32)
-    for i in range(NZ):
-        pref[i] = total
-        total = step_decay * total + got_ends[i]
-    totals[x] = total
-    for t in (xp, xm, x2):
-        remote(totals.at[x], totals.at[x], st_send.at[1], st_recv.at[1], at(x_to=t)).start()
-    w_step(2)
-    settle(totals, NX - 1, st_recv.at[1])
-    entering = jnp.zeros((1, CH), F32)
-    for i in range(NX):
-        gap = jnp.maximum(x - 1 - i, 0).astype(F32)
-        used = jnp.where(i < x, 1.0, 0.0)
-        entering = entering + used * jnp.exp(-own_rate * (float(ROWS * NZ) * gap)) * totals[i]
-    for i in range(NZ):
-        states[i] = pref[i] + jnp.exp(-own_rate * float(ROWS * i)) * entering
-    got_states[z] = states[z]
-    all_z(states, got_states, 2)
-    w_step(3)
-    w_step(4)
-    settle(got_states, NZ - 1, st_recv.at[2])
-    loads[3].wait()
-    loads[5].wait()
-    loads[6].wait()
-    coef[...] = residue[...] * jnp.sqrt(2.0 * rate[...])
+    def p_ready():
+        for key, x_from in (("p+", xm), ("p-", xp), ("p2", x2)):
+            arrived((key,), w_p.at[z, x_from])
+
+    def take_ends():
+        settle(got_ends, NZ - 1, st_recv.at[0])
+        own_rate = rate[pl.ds(z, 1), :]
+        step_decay = jnp.exp(-own_rate * float(ROWS))
+        total = jnp.zeros((1, CH), F32)
+        for i in range(NZ):
+            pref[i] = total
+            total = step_decay * total + got_ends[i]
+        totals[x] = total
+        for t in (xp, xm, x2):
+            remote(totals.at[x], totals.at[x], st_send.at[1], st_recv.at[1], at(x_to=t)).start()
+
+    def take_totals():
+        own_rate = rate[pl.ds(z, 1), :]
+        settle(totals, NX - 1, st_recv.at[1])
+        entering = jnp.zeros((1, CH), F32)
+        for i in range(NX):
+            gap = jnp.maximum(x - 1 - i, 0).astype(F32)
+            used = jnp.where(i < x, 1.0, 0.0)
+            entering = entering + used * jnp.exp(-own_rate * (float(ROWS * NZ) * gap)) * totals[i]
+        for i in range(NZ):
+            states[i] = pref[i] + jnp.exp(-own_rate * float(ROWS * i)) * entering
+        got_states[z] = states[z]
+        all_z(states, got_states, 2)
+
+    def take_states():
+        settle(got_states, NZ - 1, st_recv.at[2])
+        loads[4].wait()
+        loads[6].wait()
+        loads[7].wait()
+        coef[...] = residue[...] * jnp.sqrt(2.0 * rate[...])
 
     a_pending = []
     partner = at(ch_to=y * NC + 1 - core)
@@ -294,46 +298,89 @@
         a_copy(3, g, far, up).wait_recv()
         a_go(6, g, far, partner)
 
-    a_make(0)
-    a_make(1)
-    w_step(5)
-    a_make(2)
-    a_make(3)
-    a_pass(0)
-    w_step(6)
-    a_pass(1)
-    a_pass(2)
-    a_last(0)
-    w_step(7)
-    a_pass(3)
-    a_last(1)
-    a_last(2)
-    w_step(8)
-    a_last(3)
-    relay_step(8)
-
-    for s in range(QR + 1):
-        arrived(("x-", "r", s), q_part(back(s), xp))
-        arrived(("x2", "r", s), q_part(back(s), x2))
-    for s in range(1, QL + 1):
-        arrived(("x+", "l", s), q_part(ahead(s), xm))
-        arrived(("x2", "l", s), q_part(ahead(s), x2))
+    near = z // 2
+
+    def multiply(pair):
+        half, g = pair // GROUPS, pair % GROUPS
+        left = jnp.concatenate([a[i * NC + half, g] for i in range(NX)], axis=1)
+        for n in range(COLS // 256):
+            cols = slice(n * 256, (n + 1) * 256)
+            src, first = (w_p, 0) if n == 0 else (w_q, (n - 1) * 256)
+            right = jnp.concatenate(
+                [
+                    src[pl.ds(2 * pair, 2), i, :, first : first + 256].reshape(2 * WROWS, 256)
+                    for i in range(NX)
+                ],
+                axis=0,
+            )
+            acc[:, cols] += jnp.dot(left, right, preferred_element_type=F32)
+
+    def settled(s):
+        if s <= QR:
+            arrived(("x-", "r", s), q_part(back(s), xp))
+            arrived(("x2", "r", s), q_part(back(s), x2))
+        if 0 < s <= QL:
+            arrived(("x+", "l", s), q_part(ahead(s), xm))
+            arrived(("x2", "l", s), q_part(ahead(s), x2))
+
+    def products(n):
+        def one(i, _):
+            multiply((near + i + 8 - n) % 8)
+            return 0
+
+        lax.fori_loop(0, 2 * n + 1, one, 0)
+
+    steps = {
+        "p": p_step, "q": q_step, "r": relay_step, "m": a_make, "b": a_pass, "l": a_last,
+        "I": lambda n: p_ready(), "E": lambda n: take_ends(),
+        "T": lambda n: take_totals(), "H": lambda n: take_states(),
+        "w": lambda n: settled(n), "x": lambda n: products(n),
+    }
+
+    def run(plan):
+        for op in plan:
+            steps[op[0]](int(op[1:]))
+
+    loads[2].wait()
+    loads[3].wait()
+    pl.semaphore_wait(barrier, len(greet))
+    for n, i in enumerate(NEAR):
+        pl.semaphore_signal(
+            known.at[n], inc=1, device_id=at(z_to=(z + i) % NZ), device_id_type=MESH
+        )
+    for key, x_to in (("p+", xp), ("p-", xm), ("p2", x2)):
+        send((key,), w_p.at[z, x], at(x_to=x_to))
+    q_step(0)
+    loads[5].wait()
+    decay[...] = jnp.exp(-rate[...])
+    loads[0].wait()
+    loads[1].wait()
+    first_pass(0)
+    first_pass(1)
+    run(EARLY)
+    first_pass(2)
+    first_pass(3)
+    got_ends[z] = ends[z]
+    for n in range(len(NEAR)):
+        pl.semaphore_wait(known.at[n], 1)
+    all_z(ends, got_ends, 0)
+    run(PLAN)
+
     other = 1 - core
     for kind, block in ((0, y), (4, ym), (5, yp), (6, y2)):
         for g in range(GROUPS):
             a_copy(kind, g, block * NC + other, partner).wait_recv()
 
-    def multiply(j, _):
-        left = jnp.concatenate([a[j, g] for g in range(GROUPS)], axis=1)
-        first, x_at = (j % 2) * 8, j // 2
-        for n in range(COLS // 256):
-            cols = slice(n * 256, (n + 1) * 256)
-            right = w[pl.ds(first, 8), x_at, :, cols].reshape(8 * WROWS, 256)
-            acc[:, cols] += jnp.dot(left, right, preferred_element_type=F32)
-        return 0
-
     acc[...] = jnp.zeros_like(acc)
-    lax.fori_loop(0, NY * NC, multiply, 0)
+    for s in range(6):
+        settled(s)
+    products(2)
+    settled(6)
+    settled(7)
+    multiply((near + 3) % 8)
+    multiply((near + 5) % 8)
+    settled(8)
+    multiply((near + 4) % 8)
     out[...] = acc[...].astype(BF16)
 
     settle(got_ends, NZ - 1, st_send.at[0])
@@ -345,9 +392,9 @@
 
 def body(q_proj, k_proj, v_proj, residue, rate, skip, w_out):
     vmem = pl.BlockSpec(memory_space=pltpu.VMEM)
-    hbm = pl.BlockSpec(memory_space=pl.ANY)
+    hbm = pl.BlockSpec(memory_space=pltpu.HBM)
     dma = pltpu.SemaphoreType.DMA
-    n_w = PR + PL + QR + QL + 3 * NZ + 3
+    n_w = 2 * (PR + PL) + QR + QL + 3 * NZ + 3
     row = (1, CH)
     return pl.pallas_call(
         kernel,
@@ -361,7 +408,8 @@
             pltpu.VMEM((MODES, CH), F32),
             pltpu.VMEM((MODES, CH), F32),
             pltpu.VMEM(row, F32),
-            pltpu.VMEM((NZ, NX, WROWS, COLS), BF16),
+            pltpu.VMEM((NZ, NX, WROWS, PCOLS), BF16),
+            pltpu.VMEM((NZ, NX, WROWS, QCOLS), BF16),
             pltpu.VMEM((NY * NC, GROUPS, ROWS, 128), BF16),
             pltpu.VMEM((GROUPS, ROWS, 128), F32),
             pltpu.VMEM((ROWS, 128), F32),
@@ -375,7 +423,8 @@
             pltpu.VMEM((NZ,) + row, F32),
             pltpu.VMEM((MODES,) + row, F32),
             pltpu.VMEM((NZ,) + row, F32),
-            dma((7,)),
+            dma((8,)),
+            pltpu.SemaphoreType.REGULAR((6,)),
             dma((3,)),
             dma((3,)),
             dma((n_w,)),
@@ -384,9 +433,9 @@
             dma((7, GROUPS)),
         ],
         compiler_params=pltpu.CompilerParams(
-            collective_id=0, has_side_effects=True
+            collective_id=0, has_side_effects=True, vmem_limit_bytes=48 * 2**20
         ),
-    )(q_proj, k_proj, v_proj, w_out, residue, rate, skip.reshape(1, CH))
+    )(*[pltpu.with_memory_space_constraint(i, pltpu.HBM) for i in (q_proj, k_proj, v_proj, w_out, residue, rate, skip.reshape(1, CH))])
 
 
 def solution(mesh):

time: 71.4 us -> 63.5 us (0.89)
  Pallas kernels: 69.4 us -> 62.6 us
  local copies, waits for them, and re-layouts: 1.77 us -> 0.75 us
    pallas_call x1, Pallas kernels: 69.4 us -> 62.6 us  [body(): pl.pallas_call(kernel, out_shape=jax.ShapeDtypeStruct((ROWS, COLS), BF16)...]
    unnamed x1, local copies, waits for them, and re-layouts: 1.77 us -> 0.75 us
where the time goes in v3:
time: 63.5 us; the launch traced here: 63.4 us
  Pallas kernels  62.6 us (99%)
  local copies, waits for them, and re-layouts  0.75 us (1%)
    pallas_call x1, Pallas kernels, body(): pl.pallas_call(kernel, out_shape=jax.ShapeDtypeStruct((ROWS, COLS), BF16)...  62.6 us

profile of v3, /device:TPU:4, one launch (start us, length us, event | category | flops | bytes accessed | tf_op | source)
XLA Modules:
  0.0 63.4 jit_solution(10600396549923944887)
XLA Ops:
  0.0 62.6 %shard_map.73 = bf16[256,768]{1,0:T(8,128)(2,1)S(1)} custom-call(bf16[256,512]{1,0:T(8,128)(2,1)} %q_hbm.1, bf16[256,512]{1,0:T(8,128)(2,1)} %k_hbm.1, bf16[256,512]{1,0:T(8,128)(2,1)} %v_hbm.1, bf16[64,768]{1,0:T(8,128)(2,1)} %w_hbm.1, f32[16,512]{1,0:T(8,128)} %residue_hbm.1, f32[16,512]{1,0:T(8,128)} %rate_hbm.1, f32[1,512]{1,0:T(1,128)} %bitcast.1), custom_call_target="tpu_custom_call" | custom-call | tf_op jit(solution)/shard_map/pallas_call | solution.py:399
  62.6 0.7 %copy.9 = bf16[256,768]{1,0:T(8,128)(2,1)} copy(bf16[256,768]{1,0:T(8,128)(2,1)S(1)} %shard_map.73) | data formatting | bytes 786432

commit v4 on v3

--- a/solution.py
+++ b/solution.py
@@ -16,17 +16,17 @@
 EARLY = "".split()
 PLAN = " ".join(
     (
-        "I0 p0 q1 r0",
-        "p1 E0 q2 r1",
-        "p2 T0 q3 r2",
-        "p3 q4 r3 H0",
-        "m0 p4 m1 q5",
-        "r4 m2 p5 m3",
-        "b0 q6 r5 b1",
-        "p6 b2 l0 q7",
-        "r6 b3 l1 p7",
-        "l2 q8 r7 l3",
-        "p8 r8",
+        "I0 p0 q1 p1",
+        "r0 E0 q2 T0",
+        "p2 r1 q3 p3",
+        "r2 H0 q4 m0",
+        "p4 m1 r3 m2",
+        "q5 m3 p5 r4",
+        "b0 q6 b1 p6",
+        "r5 b2 l0 q7",
+        "b3 l1 p7 r6",
+        "l2 q8 l3 p8",
+        "r7 r8",
     )
 ).split()
 NEAR = (1, 3, 4, NZ - 4, NZ - 3, NZ - 1)

time: 63.5 us -> 62.6 us (0.986)
  Pallas kernels: 62.6 us -> 61.8 us
    pallas_call x1, Pallas kernels: 62.6 us -> 61.8 us  [body(): pl.pallas_call(kernel, out_shape=jax.ShapeDtypeStruct((ROWS, COLS), BF16)...]
where the time goes in v4:
time: 62.6 us; the launch traced here: 62.5 us
  Pallas kernels  61.8 us (99%)
  local copies, waits for them, and re-layouts  0.75 us (1%)
    pallas_call x1, Pallas kernels, body(): pl.pallas_call(kernel, out_shape=jax.ShapeDtypeStruct((ROWS, COLS), BF16)...  61.8 us

profile of v4, /device:TPU:4, one launch (start us, length us, event | category | flops | bytes accessed | tf_op | source)
XLA Modules:
  0.0 62.5 jit_solution(6574200878785974262)
XLA Ops:
  0.0 61.8 %shard_map.73 = bf16[256,768]{1,0:T(8,128)(2,1)S(1)} custom-call(bf16[256,512]{1,0:T(8,128)(2,1)} %q_hbm.1, bf16[256,512]{1,0:T(8,128)(2,1)} %k_hbm.1, bf16[256,512]{1,0:T(8,128)(2,1)} %v_hbm.1, bf16[64,768]{1,0:T(8,128)(2,1)} %w_hbm.1, f32[16,512]{1,0:T(8,128)} %residue_hbm.1, f32[16,512]{1,0:T(8,128)} %rate_hbm.1, f32[1,512]{1,0:T(1,128)} %bitcast.1), custom_call_target="tpu_custom_call" | custom-call | tf_op jit(solution)/shard_map/pallas_call | solution.py:399
  61.8 0.7 %copy.9 = bf16[256,768]{1,0:T(8,128)(2,1)} copy(bf16[256,768]{1,0:T(8,128)(2,1)S(1)} %shard_map.73) | data formatting | bytes 786432
